TPU v7x, 128 devices: a whole 4x4x4 slice. The times are simulated.
128 devices in a mesh: dp: 8 (over y, core), prompt: 16 (over x, z).
Axes of the slice: x: 4, y: 4, z: 4, core: 2. Of those that a mesh axis runs over, the one named last changes fastest.
Arguments:
- cand_hidden: bfloat16 [16, 8, 128, 1024], P('prompt', 'dp')
- ref_hidden: bfloat16 [32, 16, 128, 1024], P('dp', 'prompt')
- cand_ids: int32 [16, 8, 128], P('prompt', 'dp'), may hold values from 0 to 50264
- ref_ids: int32 [32, 16, 128], P('dp', 'prompt'), may hold values from 0 to 50264
- cand_len: int32 [16, 8], P('prompt', 'dp'), may hold values from 32 to 128
- reference_length: int32 [32, 16], P('dp', 'prompt'), may hold values from 32 to 128
- idf_table: float32 [50265], replicated, may hold values from 1 to 10
- up_weight: bfloat16 [1024, 4096], replicated, may hold values from -0.1875 to 0.1875
- up_bias: float32 [4096], replicated, may hold values from -3 to 3
- down_weight: bfloat16 [4096, 1024], replicated, may hold values from -0.09375 to 0.09375
- down_bias: float32 [1024], replicated, may hold values from -3 to 3
- norm_gain: float32 [1024], replicated, may hold values from 0.3 to 3
- norm_bias: float32 [1024], replicated, may hold values from -3 to 3
- pair_cand: int32 [8, 16, 32], P('dp', 'prompt'), may hold values from 0 to 7
- pair_ref: int32 [8, 16, 32], P('dp', 'prompt'), may hold values from 0 to 63
- pair_count: int32 [8, 16], P('dp', 'prompt'), may hold values from 8 to 32, as said below
Outputs:
- pair_scores: float32 [3, 8, 16, 32], P(None, 'dp', 'prompt')
- totals: float32 [3], replicated
Inputs may be any that keep to these rules, and one draw needn't show every extreme that they name: Slots from pair_count on are not live; some device has all 32 slots live.
All inputs are finite; a program needn't handle non-finite values.
Results may differ from a plain program's by a relative error of at most 0.0003.
Values may be sent and summed in bfloat16 or wider, within the bound.
No kernel may reach another device: no remote copies, remote signals or barrier semaphores. Data moves between devices by JAX's collectives and lax.ppermute only.
A program may use at most 128 MiB of HBM per device.

v0:
```python
import jax
import jax.numpy as jnp
from jax import lax
from jax.sharding import PartitionSpec as P


def encode_rows(hidden, up_weight, up_bias, down_weight, down_bias, norm_gain, norm_bias):
    preactivation_hidden = jnp.dot(hidden, up_weight, preferred_element_type=jnp.float32) + up_bias
    activated = jax.nn.gelu(preactivation_hidden, approximate=False).astype(jnp.bfloat16)
    summed = (
        hidden.astype(jnp.float32)
        + jnp.dot(activated, down_weight, preferred_element_type=jnp.float32)
        + down_bias
    )
    center = jnp.mean(summed, axis=-1, keepdims=True)
    spread = jnp.mean(jnp.square(summed - center), axis=-1, keepdims=True)
    normed = (summed - center) * lax.rsqrt(spread + 1e-05) * norm_gain + norm_bias
    magnitude = jnp.sum(jnp.square(normed), axis=-1, keepdims=True)
    return (normed * lax.rsqrt(magnitude + 1e-06)).astype(jnp.bfloat16)


def token_idf_weights(ids, lengths, idf_table):
    positions = jnp.arange(ids.shape[-1], dtype=jnp.int32)
    live_tokens = positions[None, :] < lengths[:, None]
    return jnp.where(live_tokens, jnp.take(idf_table, ids, axis=0), 0.0).astype(jnp.bfloat16)


def on_device(
    cand_hidden,
    ref_hidden,
    cand_ids,
    ref_ids,
    cand_len,
    reference_length,
    idf_table,
    up_weight,
    up_bias,
    down_weight,
    down_bias,
    norm_gain,
    norm_bias,
    pair_cand,
    pair_ref,
    pair_count,
):
    seq_len = cand_hidden.shape[2]
    width = cand_hidden.shape[3]

    def encode_side(hidden, ids, lengths):
        units = encode_rows(
            hidden.reshape(-1, width),
            up_weight,
            up_bias,
            down_weight,
            down_bias,
            norm_gain,
            norm_bias,
        )
        weights = token_idf_weights(ids.reshape(-1, seq_len), lengths.reshape(-1), idf_table)
        return (units.reshape(hidden.shape), weights.reshape(hidden.shape[:3]))

    ref_unit, ref_weight = encode_side(ref_hidden, ref_ids, reference_length)
    candidate_normalized, cand_weight = encode_side(cand_hidden, cand_ids, cand_len)
    cand_all, cand_wall = (
        lax.all_gather(candidate_normalized, "dp", axis=1, tiled=True),
        lax.all_gather(cand_weight, "dp", axis=1, tiled=True),
    )
    cand_all = cand_all.reshape(-1, seq_len, width)
    cand_wall = cand_wall.reshape(-1, seq_len)
    cand_pick = pair_cand.reshape(-1)
    slot_total = cand_pick.shape[0]
    ref_pick = pair_ref.reshape(-1)
    groups = lax.axis_size("prompt")
    ref_major = ref_pick // groups
    ref_minor = ref_pick % groups
    order = jnp.argsort(ref_minor, stable=True)
    sorted_minor = jnp.take(ref_minor, order, axis=0)
    sorted_major = jnp.take(ref_major, order, axis=0)
    sorted_cand = jnp.take(cand_pick, order, axis=0)
    paired_normalized = jnp.take(cand_all, sorted_cand, axis=0)
    pair_weight = jnp.take(cand_wall, sorted_cand, axis=0)
    initial = (
        jnp.zeros((slot_total, seq_len), jnp.float32),
        jnp.zeros((slot_total, seq_len), jnp.float32),
        jnp.zeros((slot_total, seq_len), jnp.bfloat16),
    )
    ref_all, ref_wall = (
        lax.all_gather(ref_unit, "prompt", axis=1, tiled=True),
        lax.all_gather(ref_weight, "prompt", axis=1, tiled=True),
    )
    shard_span = ref_all.shape[1]
    inside = (sorted_minor >= 0) & (sorted_minor < 0 + shard_span)
    within = sorted_major * shard_span + jnp.clip(sorted_minor - 0, 0, shard_span - 1)
    selected_normalized = jnp.take(ref_all.reshape(-1, seq_len, width), within, axis=0)
    chosen_weight = jnp.take(ref_wall.reshape(-1, seq_len), within, axis=0)
    cosine_similarity = jnp.einsum(
        "uqg,uog->uqo", paired_normalized, selected_normalized, preferred_element_type=jnp.float32
    )
    row_best = jnp.max(
        jnp.where(chosen_weight[:, None, :] > 0, cosine_similarity, -10000.0), axis=2
    )
    col_best = jnp.max(jnp.where(pair_weight[:, :, None] > 0, cosine_similarity, -10000.0), axis=1)
    keeper = inside[:, None]
    updated = []
    for stored, fresh in zip(initial, (row_best, col_best, chosen_weight)):
        updated.append(jnp.where(keeper, fresh, stored))
    row_best, col_best, ref_chosen = tuple(updated)
    cand_float = pair_weight.astype(jnp.float32)
    ref_float = ref_chosen.astype(jnp.float32)
    precision_sorted = jnp.sum(cand_float * row_best, axis=1) / jnp.sum(cand_float, axis=1)
    recall_sorted = jnp.sum(ref_float * col_best, axis=1) / jnp.sum(ref_float, axis=1)
    inverse = jnp.argsort(order)
    precision = jnp.take(precision_sorted, inverse, axis=0)
    recall = jnp.take(recall_sorted, inverse, axis=0)
    fmeasure = 2.0 * precision * recall / jnp.maximum(precision + recall, 0.7)
    live_slots = jnp.arange(slot_total, dtype=jnp.int32) < pair_count.reshape(1)
    stacked = jnp.where(live_slots[None, :], jnp.stack([precision, recall, fmeasure]), 0.0)
    score_sums, live_total = lax.psum(
        (jnp.sum(stacked, axis=1), jnp.sum(live_slots.astype(jnp.float32))), ("dp", "prompt")
    )
    return (stacked.reshape(3, 1, 1, slot_total), score_sums / live_total)


def solution(mesh):
    placed = (
        P("prompt", "dp", None, None),
        P("dp", "prompt", None, None),
        P("prompt", "dp", None),
        P("dp", "prompt", None),
        P("prompt", "dp"),
        P("dp", "prompt"),
        P(),
        P(),
        P(),
        P(),
        P(),
        P(),
        P(),
        P("dp", "prompt", None),
        P("dp", "prompt", None),
        P("dp", "prompt"),
    )
    return jax.shard_map(
        on_device,
        mesh=mesh,
        in_specs=placed,
        out_specs=(P(None, "dp", "prompt", None), P()),
        check_vma=False,
    )
```

profile of v0, /device:TPU:1, one launch (start us, length us, event | category | flops | bytes accessed | tf_op | source)
XLA Modules:
  0.0 263.4 jit_solution(12290140118969234346)
XLA Ops:
  7.2 13.2 %fusion.169 = (f32[128]{0:T(128)S(1)}, f32[128,1024]{1,0:T(8,128)S(1)}) fusion(f32[1024]{0:T(1024)} %param.30, bf16[4096,1024]{1,0:T(8,128)(2,1)} %param.29, bf16[1024,4096]{1,0:T(8,128)(2,1)} %param.27, f32[4096]{0:T(1024)} %param.28, bf16[1,1,128,1024]{3,2,1,0:T(8,128)(2,1)} %param.20), kind=kOutput, calls=%fused_computation.264 | convolution fusion | flops 2182610944 | bytes 17584640 | tf_op jit(solution)/shard_map/dot_general | solution.py:12
  21.0 0.9 multiply_convert_fusion.1
  22.2 30.3 %fusion.168 = (f32[512]{0:T(512)S(1)}, f32[512,1024]{1,0:T(8,128)S(1)}) fusion(f32[1024]{0:T(1024)S(1)} %copy-done.9, bf16[4096,1024]{1,0:T(8,128)(2,1)} %param.29, bf16[512,1024]{1,0:T(8,128)(2,1)S(1)} %bitcast.84, bf16[1024,4096]{1,0:T(8,128)(2,1)} %param.27, f32[4096]{0:T(1024)S(1)} %copy-done.8), kind=kOutput, calls=%fused_computation.263 | convolution fusion | flops 8730443776 | bytes 19945472 | tf_op jit(solution)/shard_map/dot_general | solution.py:12
  52.8 0.9 multiply_reduce_fusion
  53.8 1.5 multiply_convert_fusion
  56.6 1.1 gather_fusion
  57.8 12.1 %all_gather.12 = bf16[1,8,128]{2,0,1:T(2,128)(2,1)S(1)} all-gather(bf16[1,1,128]{2,0,1:T(2,128)(2,1)S(1)} %fusion.100), channel_id=1, replica_groups=mesh['dp'=8,'prompt'=16] {'dp'}, dimensions={1}, use_global_device_ids=true | all-gather | bytes 2304 | tf_op jit(solution)/shard_map/all_gather | solution.py:66
  69.9 1.6 sort.34
  71.5 0.7 gather_fusion.7
  72.2 0.7 gather_fusion.8
  72.9 0.7 gather_fusion.6
  73.6 3.1 %gather_fusion.2 = bf16[512]{0:T(512)(128)(2,1)S(1)} fusion(f32[50265]{0:T(1024)S(1)} %copy-done, s32[1024]{0:T(1024)S(1)} %pad_clamp_fusion.2), kind=kCustom, calls=%fused_computation.7 | custom fusion | bytes 4096 | tf_op jit(solution)/shard_map/jit(_take)/gather | solution.py:25
  76.8 20.3 %all_gather.13 = bf16[4,16,128]{2,0,1:T(4,128)(2,1)S(1)} all-gather(bf16[4,1,128]{2,0,1:T(4,128)(2,1)S(1)} %fusion.98), channel_id=1, replica_groups=mesh['dp'=8,'prompt'=16] {'prompt'}, dimensions={1}, use_global_device_ids=true | all-gather | bytes 17408 | tf_op jit(solution)/shard_map/all_gather | solution.py:89
  97.2 1.6 sort.35
  98.8 0.6 convert_reduce_fusion.2
  99.4 0.6 gather_fusion.1
  100.8 6.9 %gather_fusion.4 = bf16[32,128,1024]{2,1,0:T(8,128)(2,1)} fusion(bf16[8,128,1024]{2,1,0:T(8,128)(2,1)} %bitcast.74, s32[1024]{0:T(1024)S(1)} %get-tuple-element.39), kind=kCustom, calls=%fused_computation.9 | custom fusion | bytes 16777344 | tf_op jit(solution)/shard_map/jit(_take)/gather | solution.py:80
  107.7 62.4 %all-gather.4.cloned.1.call-done = bf16[4,16,128,1024]{3,2,1,0:T(8,128)(2,1)} async-done(((bf16[4,1,128,1024]{3,2,1,0:T(8,128)(2,1)}), bf16[4,16,128,1024]{3,2,1,0:T(8,128)(2,1)}) %all-gather.4.cloned.1.call-update) | async-done | bytes 16777232 | tf_op jit(solution)/shard_map/all_gather | solution.py:88
  170.1 10.8 %gather_fusion.5 = bf16[32,128,1024]{2,1,0:T(8,128)(2,1)} fusion(bf16[64,128,1024]{2,1,0:T(8,128)(2,1)} %bitcast.75, s32[1024]{0:T(1024)S(1)} %get-tuple-element.38), kind=kCustom, calls=%fused_computation.10 | custom fusion | bytes 16777344 | tf_op jit(solution)/shard_map/jit(_take)/gather | solution.py:94
  180.8 7.5 %select_reduce_fusion = (f32[32,128]{1,0:T(8,128)S(1)}, f32[32,128]{1,0:T(8,128)S(1)}) fusion(pred[32,128]{1,0:T(8,128)(4,1)S(1)} %broadcast_compare_fusion, pred[32,128]{1,0:T(8,128)(4,1)S(1)} %broadcast_compare_fusion.1, bf16[32,128,1024]{2,1,0:T(8,128)(2,1)} %gather_fusion.5, pred[32]{0:T(512)(128)(4,1)S(1)} %get-tuple-element.22, ...), kind=kOutput, calls=%fused_computation.73 | convolution fusion | flops 1084219392 | bytes 16818240 | tf_op jit(solution)/shard_map/uqg,uog->uqo/dot_general | solution.py:96
  188.6 0.7 gather_fusion.9
  189.3 0.7 gather_fusion.10
  190.2 64.7 %all-reduce = (f32[3]{0:T(128)S(1)}, f32[]{:T(128)}) all-reduce(f32[3]{0:T(128)S(1)} %fusion.96, f32[]{:T(128)} %convert_reduce_fusion.2), channel_id=1, replica_groups=mesh['dp'=8,'prompt'=16] {'dp','prompt'}, use_global_device_ids=true, to_apply=%region_15.18 | all-reduce | flops 4 | bytes 32 | tf_op jit(solution)/shard_map/psum | solution.py:118
  254.9 1.2 broadcast_divide_fusion
  (65 shorter events, 3.1 us)
Async XLA Ops:
  7.2 49.4 %copy-start = (f32[50265]{0:T(1024)S(1)}, f32[50265]{0:T(1024)}, u32[]{:S(2)}) copy-start(f32[50265]{0:T(1024)} %param.26) | copy-start | bytes 603184
  7.2 13.5 %copy-start.2 = (f32[1024]{0:T(1024)S(1)}, f32[1024]{0:T(1024)}, u32[]{:S(2)}) copy-start(f32[1024]{0:T(1024)} %param.32) | copy-start | bytes 12292
  7.2 13.5 %copy-start.3 = (f32[1024]{0:T(1024)S(1)}, f32[1024]{0:T(1024)}, u32[]{:S(2)}) copy-start(f32[1024]{0:T(1024)} %param.31) | copy-start | bytes 12292
  7.2 93.6 %all-gather.6.cloned.1.call-start = ((), (), s32[]{:S(2)}) async-start(), calls=%async_computation.1 | async-start | bytes 2359296 | tf_op jit(solution)/shard_map/all_gather | solution.py:65
  20.5 1.7 copy-start.7
  20.5 1.7 copy-start.8
  20.5 1.7 copy-start.9
  21.9 148.1 %all-gather.4.cloned.1.call-start = ((), (), s32[]{:S(2)}) async-start(), calls=%async_computation | async-start | bytes 17825792 | tf_op jit(solution)/shard_map/all_gather | solution.py:88
  53.7 2.8 %copy-start.6 = (s32[1,1,128]{2,1,0:T(1,128)S(1)}, s32[1,1,128]{2,1,0:T(1,128)}, u32[]{:S(2)}) copy-start(s32[1,1,128]{2,1,0:T(1,128)} %param.22) | copy-start | bytes 1540
  53.7 16.1 %copy-start.10 = (s32[1,1,32]{2,1,0:T(1,128)S(1)}, s32[1,1,32]{2,1,0:T(1,128)}, u32[]{:S(2)}) copy-start(s32[1,1,32]{2,1,0:T(1,128)} %param.34) | copy-start | bytes 388
  55.2 17.7 %copy-start.1 = (s32[1,1,32]{2,1,0:T(1,128)S(1)}, s32[1,1,32]{2,1,0:T(1,128)}, u32[]{:S(2)}) copy-start(s32[1,1,32]{2,1,0:T(1,128)} %param.33) | copy-start | bytes 388
  55.2 18.4 %copy-start.4 = (s32[4,1,128]{2,1,0:T(1,128)S(1)}, s32[4,1,128]{2,1,0:T(1,128)}, u32[]{:S(2)}) copy-start(s32[4,1,128]{2,1,0:T(1,128)} %param.23) | copy-start | bytes 6148
  55.2 21.6 %copy-start.5 = (s32[4,1]{0,1:T(1,128)S(1)}, s32[4,1]{0,1:T(1,128)}, u32[]{:S(2)}) copy-start(s32[4,1]{0,1:T(1,128)} %param.25) | copy-start | bytes 52
Sparse Core Ops, SparseCore 0:
  22.0 28.8 all-gather.5
  55.4 114.6 all-gather.3
where the time goes:
time: 264 us; the launch traced here: 263 us
  blocking collectives  97 us (37%)
  waiting for transfers between devices  62.4 us (24%)
  matrix products  51 us (19%)
  local copies, waits for them, and re-layouts  26.7 us (10%)
  between operations  15.6 us (6%)
  other arithmetic  10.3 us (4%)
    psum x1, blocking collectives, on_device(): lax.psum((jnp.sum(stacked, axis=1), jnp.sum(live_slots.astype(jnp.float32...  64.7 us
    all_gather x1, waiting for transfers between devices, on_device(): lax.all_gather(ref_unit, 'prompt', axis=1, tiled=True)  62.4 us
    dot_general x2, matrix products, encode_rows(): jnp.dot(activated, down_weight, preferred_element_type=jnp.float32)  43.5 us
    all_gather x1, blocking collectives, on_device(): lax.all_gather(ref_weight, 'prompt', axis=1, tiled=True)  20.3 us
    all_gather x1, blocking collectives, on_device(): lax.all_gather(cand_weight, 'dp', axis=1, tiled=True)  12.1 us
    gather x1, local copies, waits for them, and re-layouts, on_device(): jnp.take(ref_all.reshape(-1, seq_len, width), within, axis=0)  10.8 us
    dot_general x1, matrix products, on_device(): jnp.einsum('uqg,uog->uqo', paired_normalized, selected_normalized, prefer...  7.55 us
    gather x1, local copies, waits for them, and re-layouts, on_device(): paired_normalized = jnp.take(cand_all, sorted_cand, axis=0)  6.87 us
  transfers between devices with their start and end apart: 2, of which 1 were waited for; matrix products, arithmetic and copies ran while one was open for 20% of the time, Pallas kernels for 0%

commit v1 on v0

--- a/solution.py
+++ b/solution.py
@@ -116,7 +116,8 @@
     live_slots = jnp.arange(slot_total, dtype=jnp.int32) < pair_count.reshape(1)
     stacked = jnp.where(live_slots[None, :], jnp.stack([precision, recall, fmeasure]), 0.0)
     score_sums, live_total = lax.psum(
-        (jnp.sum(stacked, axis=1), jnp.sum(live_slots.astype(jnp.float32))), ("dp", "prompt")
+        lax.psum((jnp.sum(stacked, axis=1), jnp.sum(live_slots.astype(jnp.float32))), "prompt"),
+        "dp",
     )
     return (stacked.reshape(3, 1, 1, slot_total), score_sums / live_total)
 

time: 264 us -> 251 us (0.951)
  blocking collectives: 97 us -> 84.5 us
    psum x1, blocking collectives: 64.7 us -> 32.2 us  [on_device(): lax.psum((jnp.sum(stacked, axis=1), jnp.sum(live_slots.astype(jnp.float32...]
    psum x0 -> x1, blocking collectives: none -> 20 us  [on_device(): lax.psum(lax.psum((jnp.sum(stacked, axis=1), jnp.sum(live_slots.astype(jn...]
  transfers between devices with their start and end apart: 2 -> 2, of which waited for: 1 -> 1; matrix products, arithmetic and copies ran while one was open for 20% -> 21% of each run, Pallas kernels for 0% -> 0%
where the time goes in v1:
time: 251 us
  blocking collectives  84.5 us (34%)
  waiting for transfers between devices  62.4 us (25%)
  matrix products  51 us (20%)
  local copies, waits for them, and re-layouts  26.7 us (11%)
  between operations  15.6 us (6%)
  other arithmetic  10.3 us (4%)
    all_gather x1, waiting for transfers between devices, on_device(): lax.all_gather(ref_unit, 'prompt', axis=1, tiled=True)  62.4 us
    dot_general x2, matrix products, encode_rows(): jnp.dot(activated, down_weight, preferred_element_type=jnp.float32)  43.5 us
    psum x1, blocking collectives, on_device(): lax.psum((jnp.sum(stacked, axis=1), jnp.sum(live_slots.astype(jnp.float32...  32.2 us
    all_gather x1, blocking collectives, on_device(): lax.all_gather(ref_weight, 'prompt', axis=1, tiled=True)  20.3 us
    psum x1, blocking collectives, on_device(): lax.psum(lax.psum((jnp.sum(stacked, axis=1), jnp.sum(live_slots.astype(jn...  20 us
    all_gather x1, blocking collectives, on_device(): lax.all_gather(cand_weight, 'dp', axis=1, tiled=True)  12.1 us
    gather x1, local copies, waits for them, and re-layouts, on_device(): jnp.take(ref_all.reshape(-1, seq_len, width), within, axis=0)  10.8 us
    dot_general x1, matrix products, on_device(): jnp.einsum('uqg,uog->uqo', paired_normalized, selected_normalized, prefer...  7.55 us
  transfers between devices with their start and end apart: 2, of which 1 were waited for; matrix products, arithmetic and copies ran while one was open for 21% of the time, Pallas kernels for 0%

profile of v1, /device:TPU:1, one launch (start us, length us, event | category | flops | bytes accessed | tf_op | source)
XLA Modules:
  0.0 250.9 jit_solution(16127311340115645470)
XLA Ops:
  7.2 13.2 %fusion.169 = (f32[128]{0:T(128)S(1)}, f32[128,1024]{1,0:T(8,128)S(1)}) fusion(f32[1024]{0:T(1024)} %param.30, bf16[4096,1024]{1,0:T(8,128)(2,1)} %param.29, bf16[1024,4096]{1,0:T(8,128)(2,1)} %param.27, f32[4096]{0:T(1024)} %param.28, bf16[1,1,128,1024]{3,2,1,0:T(8,128)(2,1)} %param.20), kind=kOutput, calls=%fused_computation.264 | convolution fusion | flops 2182610944 | bytes 17584640 | tf_op jit(solution)/shard_map/dot_general | solution.py:12
  21.0 0.9 multiply_convert_fusion.1
  22.2 30.3 %fusion.168 = (f32[512]{0:T(512)S(1)}, f32[512,1024]{1,0:T(8,128)S(1)}) fusion(f32[1024]{0:T(1024)S(1)} %copy-done.9, bf16[4096,1024]{1,0:T(8,128)(2,1)} %param.29, bf16[512,1024]{1,0:T(8,128)(2,1)S(1)} %bitcast.84, bf16[1024,4096]{1,0:T(8,128)(2,1)} %param.27, f32[4096]{0:T(1024)S(1)} %copy-done.8), kind=kOutput, calls=%fused_computation.263 | convolution fusion | flops 8730443776 | bytes 19945472 | tf_op jit(solution)/shard_map/dot_general | solution.py:12
  52.8 0.9 multiply_reduce_fusion
  53.7 1.5 multiply_convert_fusion
  56.6 1.1 gather_fusion
  57.8 12.1 %all_gather.12 = bf16[1,8,128]{2,0,1:T(2,128)(2,1)S(1)} all-gather(bf16[1,1,128]{2,0,1:T(2,128)(2,1)S(1)} %fusion.100), channel_id=1, replica_groups=mesh['dp'=8,'prompt'=16] {'dp'}, dimensions={1}, use_global_device_ids=true | all-gather | bytes 2304 | tf_op jit(solution)/shard_map/all_gather | solution.py:66
  69.8 1.6 sort.34
  71.5 0.7 gather_fusion.7
  72.2 0.7 gather_fusion.8
  72.9 0.7 gather_fusion.6
  73.6 3.1 %gather_fusion.2 = bf16[512]{0:T(512)(128)(2,1)S(1)} fusion(f32[50265]{0:T(1024)S(1)} %copy-done, s32[1024]{0:T(1024)S(1)} %pad_clamp_fusion.2), kind=kCustom, calls=%fused_computation.7 | custom fusion | bytes 4096 | tf_op jit(solution)/shard_map/jit(_take)/gather | solution.py:25
  76.8 20.3 %all_gather.13 = bf16[4,16,128]{2,0,1:T(4,128)(2,1)S(1)} all-gather(bf16[4,1,128]{2,0,1:T(4,128)(2,1)S(1)} %fusion.98), channel_id=1, replica_groups=mesh['dp'=8,'prompt'=16] {'prompt'}, dimensions={1}, use_global_device_ids=true | all-gather | bytes 17408 | tf_op jit(solution)/shard_map/all_gather | solution.py:89
  97.2 1.6 sort.35
  98.8 0.6 convert_reduce_fusion.2
  100.8 6.9 %gather_fusion.4 = bf16[32,128,1024]{2,1,0:T(8,128)(2,1)} fusion(bf16[8,128,1024]{2,1,0:T(8,128)(2,1)} %bitcast.74, s32[1024]{0:T(1024)S(1)} %get-tuple-element.41), kind=kCustom, calls=%fused_computation.9 | custom fusion | bytes 16777344 | tf_op jit(solution)/shard_map/jit(_take)/gather | solution.py:80
  107.7 62.4 %all-gather.4.cloned.1.call-done = bf16[4,16,128,1024]{3,2,1,0:T(8,128)(2,1)} async-done(((bf16[4,1,128,1024]{3,2,1,0:T(8,128)(2,1)}), bf16[4,16,128,1024]{3,2,1,0:T(8,128)(2,1)}) %all-gather.4.cloned.1.call-update) | async-done | bytes 16777232 | tf_op jit(solution)/shard_map/all_gather | solution.py:88
  170.1 10.8 %gather_fusion.5 = bf16[32,128,1024]{2,1,0:T(8,128)(2,1)} fusion(bf16[64,128,1024]{2,1,0:T(8,128)(2,1)} %bitcast.75, s32[1024]{0:T(1024)S(1)} %get-tuple-element.40), kind=kCustom, calls=%fused_computation.10 | custom fusion | bytes 16777344 | tf_op jit(solution)/shard_map/jit(_take)/gather | solution.py:94
  180.8 7.6 %select_reduce_fusion = (f32[32,128]{1,0:T(8,128)S(1)}, f32[32,128]{1,0:T(8,128)S(1)}) fusion(pred[32,128]{1,0:T(8,128)(4,1)S(1)} %broadcast_compare_fusion, pred[32,128]{1,0:T(8,128)(4,1)S(1)} %broadcast_compare_fusion.1, bf16[32,128,1024]{2,1,0:T(8,128)(2,1)} %gather_fusion.5, pred[32]{0:T(512)(128)(4,1)S(1)} %get-tuple-element.24, ...), kind=kOutput, calls=%fused_computation.73 | convolution fusion | flops 1084219392 | bytes 16818240 | tf_op jit(solution)/shard_map/uqg,uog->uqo/dot_general | solution.py:96
  188.6 0.7 gather_fusion.9
  189.3 0.7 gather_fusion.10
  190.2 32.2 %all-reduce = (f32[3]{0:T(128)S(1)}, f32[]{:T(128)}) all-reduce(f32[3]{0:T(128)S(1)} %fusion.96, f32[]{:T(128)} %convert_reduce_fusion.2), channel_id=1, replica_groups=mesh['dp'=8,'prompt'=16] {'prompt'}, use_global_device_ids=true, to_apply=%region_15.18 | all-reduce | flops 4 | bytes 32 | tf_op jit(solution)/shard_map/psum | solution.py:119
  222.4 20.0 %all-reduce.1 = (f32[3]{0:T(128)S(1)}, f32[]{:T(128)}) all-reduce(f32[3]{0:T(128)S(1)} %get-tuple-element.16, f32[]{:T(128)} %get-tuple-element.17), channel_id=1, replica_groups=mesh['dp'=8,'prompt'=16] {'dp'}, use_global_device_ids=true, to_apply=%region_16.19 | all-reduce | flops 4 | bytes 32 | tf_op jit(solution)/shard_map/psum | solution.py:118
  242.4 1.2 broadcast_divide_fusion
  (66 shorter events, 3.7 us)
Async XLA Ops:
  7.2 49.4 %copy-start = (f32[50265]{0:T(1024)S(1)}, f32[50265]{0:T(1024)}, u32[]{:S(2)}) copy-start(f32[50265]{0:T(1024)} %param.26) | copy-start | bytes 603184
  7.2 13.5 %copy-start.2 = (f32[1024]{0:T(1024)S(1)}, f32[1024]{0:T(1024)}, u32[]{:S(2)}) copy-start(f32[1024]{0:T(1024)} %param.32) | copy-start | bytes 12292
  7.2 13.5 %copy-start.3 = (f32[1024]{0:T(1024)S(1)}, f32[1024]{0:T(1024)}, u32[]{:S(2)}) copy-start(f32[1024]{0:T(1024)} %param.31) | copy-start | bytes 12292
  7.2 93.6 %all-gather.6.cloned.1.call-start = ((), (), s32[]{:S(2)}) async-start(), calls=%async_computation.1 | async-start | bytes 2359296 | tf_op jit(solution)/shard_map/all_gather | solution.py:65
  20.5 1.7 copy-start.7
  20.5 1.7 copy-start.8
  20.5 1.7 copy-start.9
  21.9 148.1 %all-gather.4.cloned.1.call-start = ((), (), s32[]{:S(2)}) async-start(), calls=%async_computation | async-start | bytes 17825792 | tf_op jit(solution)/shard_map/all_gather | solution.py:88
  53.7 2.8 %copy-start.6 = (s32[1,1,128]{2,1,0:T(1,128)S(1)}, s32[1,1,128]{2,1,0:T(1,128)}, u32[]{:S(2)}) copy-start(s32[1,1,128]{2,1,0:T(1,128)} %param.22) | copy-start | bytes 1540
  53.7 16.1 %copy-start.10 = (s32[1,1,32]{2,1,0:T(1,128)S(1)}, s32[1,1,32]{2,1,0:T(1,128)}, u32[]{:S(2)}) copy-start(s32[1,1,32]{2,1,0:T(1,128)} %param.34) | copy-start | bytes 388
  55.2 17.7 %copy-start.1 = (s32[1,1,32]{2,1,0:T(1,128)S(1)}, s32[1,1,32]{2,1,0:T(1,128)}, u32[]{:S(2)}) copy-start(s32[1,1,32]{2,1,0:T(1,128)} %param.33) | copy-start | bytes 388
  55.2 18.4 %copy-start.4 = (s32[4,1,128]{2,1,0:T(1,128)S(1)}, s32[4,1,128]{2,1,0:T(1,128)}, u32[]{:S(2)}) copy-start(s32[4,1,128]{2,1,0:T(1,128)} %param.23) | copy-start | bytes 6148
  55.2 21.6 %copy-start.5 = (s32[4,1]{0,1:T(1,128)S(1)}, s32[4,1]{0,1:T(1,128)}, u32[]{:S(2)}) copy-start(s32[4,1]{0,1:T(1,128)} %param.25) | copy-start | bytes 52
Sparse Core Ops, SparseCore 0:
  22.0 28.8 all-gather.5
  55.3 114.6 all-gather.3
